TPU v7x, 32 devices: a whole 2x2x4 slice. The times are simulated.
32 devices in a mesh: groups: 2 (over y), seq: 4 (over z), ep: 2 (over x), tp: 2 (over core).
Axes of the slice: x: 2, y: 2, z: 4, core: 2. Of those that a mesh axis runs over, the one named last changes fastest.
Arguments:
- hidden: bfloat16 [2048, 1440], P(('groups', 'seq', 'ep')), parts along dimension 0, may hold values from -6 to 6
- expert_ids: int32 [2048, 4], P(('groups', 'seq', 'ep')), parts along dimension 0, may hold values from 0 to 7, all different within a row; in each aligned block of 128 rows (0 to 127, 128 to 255, ...) at most 88 rows name the same one
- gate_units: int32 [2048, 4], P(('groups', 'seq', 'ep')), parts along dimension 0, may hold values from 4096 to 32767
- w_gate: bfloat16 [8, 1440, 1440], P(('seq', 'tp'), None, 'ep'), may hold values from -0.15625 to 0.15625
- w_up: bfloat16 [8, 1440, 1440], P(('seq', 'tp'), None, 'ep'), may hold values from -0.15625 to 0.15625
- w_down: bfloat16 [8, 1440, 1440], P(('seq', 'tp'), None, 'ep'), may hold values from -0.15625 to 0.15625
Outputs:
- moe_out: bfloat16 [2048, 1440], P(('groups', 'seq', 'ep'), 'tp'), parts along dimension 0
There are 2 independent parts, one for each index of `groups`. A program takes and returns all parts, laid end to end along the dimension named above; an argument that names none is the same for every part. Nothing has to cross between parts.
Inputs may be any that keep to these rules, and one draw needn't show every extreme that they name: `expert_ids`: each row names 4 different experts; in each aligned block of 128 rows no expert is named by more than 88 rows, and in every draw some expert is named by exactly 88 rows of some block.
All inputs are finite; a program needn't handle non-finite values.
Results may differ from a plain program's by a relative error of at most 0.0064.
Values may be sent and summed in bfloat16 or wider, within the bound.
A program may use at most 64 MiB of HBM per device.

v0:
```python
import jax
import jax.numpy as jnp
from jax import lax
from jax.sharding import PartitionSpec as P

TOP = 4


def slice_output(rows_in, gate_cols, up_cols, down_cols):
    gate_pre = jnp.dot(rows_in, gate_cols, preferred_element_type=jnp.float32)
    up_pre = jnp.dot(rows_in, up_cols, preferred_element_type=jnp.float32)
    activation = ((up_pre + 1.0) * gate_pre * jax.nn.sigmoid(1.702 * gate_pre)).astype(jnp.bfloat16)
    return lax.dot_general(
        activation, down_cols, (((1,), (1,)), ((), ())), preferred_element_type=jnp.float32
    ).astype(jnp.bfloat16)


def local(hidden, expert_ids, gate_units, w_gate, w_up, w_down):
    token_count, model_width = hidden.shape
    seq_count = lax.axis_size("seq")
    ep_count = lax.axis_size("ep")
    tp_count = lax.axis_size("tp")
    half_width = model_width // tp_count
    my_half = lax.axis_index("tp")
    expert_count = seq_count * tp_count
    capacity = max(2, (token_count * TOP * 11 + expert_count * 8 - 1) // (expert_count * 8))
    flat_ids = expert_ids.reshape(-1)
    onehot_ids = (flat_ids[:, None] == jnp.arange(expert_count, dtype=jnp.int32)[None, :]).astype(
        jnp.int32
    )
    slot_rank = jnp.sum((jnp.cumsum(onehot_ids, axis=0) - 1) * onehot_ids, axis=1)
    owner_seq = flat_ids // tp_count
    owner_half = flat_ids % tp_count
    send_row = jnp.where(owner_half == my_half, owner_seq * capacity + slot_rank, -1)
    selector = jnp.arange(seq_count * capacity, dtype=jnp.int32)[:, None] == send_row[None, :]
    selector = jnp.any(selector.reshape(seq_count * capacity, token_count, TOP), axis=2).astype(
        jnp.bfloat16
    )
    outgoing = jnp.dot(selector, hidden, preferred_element_type=jnp.float32).astype(jnp.bfloat16)
    outgoing = outgoing.reshape(seq_count, capacity, model_width)
    column_of = (owner_half * seq_count + owner_seq) * capacity + slot_rank
    gate_share = gate_units.reshape(-1).astype(jnp.float32) / 65536.0
    column_ids = jnp.arange(tp_count * seq_count * capacity, dtype=jnp.int32)
    combiner = jnp.where(column_ids[None, :] == column_of[:, None], gate_share[:, None], 0.0)
    combiner = jnp.sum(combiner.reshape(token_count, TOP, -1), axis=1)
    copied = jnp.broadcast_to(outgoing[:, None], (seq_count, ep_count, capacity, model_width))
    copied = copied.reshape(seq_count * ep_count, capacity, model_width)
    arrived = lax.all_to_all(copied, ("seq", "ep"), split_axis=0, concat_axis=0, tiled=True)
    slice_rows = slice_output(arrived.reshape(-1, model_width), w_gate[0], w_up[0], w_down[0])
    slice_rows = slice_rows.reshape(seq_count * ep_count, capacity, model_width)
    came_back = lax.all_to_all(
        lax.all_to_all(slice_rows, ("seq", "ep"), split_axis=0, concat_axis=0, tiled=True),
        "tp",
        split_axis=2,
        concat_axis=0,
        tiled=True,
    )
    came_back = came_back.reshape(tp_count, seq_count, ep_count, capacity, half_width)
    returned = jnp.sum(came_back.astype(jnp.float32), axis=2).astype(jnp.bfloat16)
    result_rows = returned.reshape(-1, half_width).astype(jnp.float32)
    moe_out = jnp.dot(
        combiner, result_rows, precision=lax.Precision.HIGHEST, preferred_element_type=jnp.float32
    )
    return moe_out.astype(jnp.bfloat16)


def solution(mesh):
    return jax.shard_map(
        local,
        mesh=mesh,
        in_specs=(
            P(("groups", "seq", "ep"), None),
            P(("groups", "seq", "ep"), None),
            P(("groups", "seq", "ep"), None),
            P(("seq", "tp"), None, "ep"),
            P(("seq", "tp"), None, "ep"),
            P(("seq", "tp"), None, "ep"),
        ),
        out_specs=P(("groups", "seq", "ep"), "tp"),
        check_vma=False,
    )
```

profile of v0, /device:TPU:0, one launch (start us, length us, event | category | flops | bytes accessed | tf_op | source)
XLA Modules:
  0.0 157.3 jit_solution(9115896044357004231)
XLA Ops:
  0.0 0.0 copy-start
  0.0 0.9 copy.72
  0.9 0.1 eq.70
  1.0 0.1 eq.66
  1.2 1.1 reduce-window.6
  2.3 0.2 slice_reduce_fusion
  2.6 0.1 fusion.10
  2.7 0.1 reduce_sum.33
  2.8 0.1 copy.74
  2.8 0.7 add_select_fusion.2
  3.6 0.1 fusion.9
  3.7 1.4 convolution_convert_fusion.1
  5.1 0.2 broadcast_in_dim.30
  5.3 0.0 copy-start.3
  5.3 57.4 %all_to_all.25 = bf16[8,88,1440]{2,1,0:T(8,128)(2,1)S(1)} all-to-all(bf16[8,88,1440]{2,1,0:T(8,128)(2,1)S(1)} %bitcast.36), channel_id=1, replica_groups=mesh['groups'=2,'seq'=4,'ep'=2,'tp'=2] {'seq','ep'}, dimensions={0} | all-to-all | bytes 4055040 | tf_op jit(solution)/shard_map/all_to_all | solution.py:48
  62.7 0.0 copy-start.1
  62.7 1.3 copy-done.1
  64.1 0.0 copy-done.3
  64.1 3.2 %fusion.1 = f32[704,720]{1,0:T(8,128)} fusion(bf16[704,1440]{1,0:T(8,128)(2,1)S(1)} %bitcast.40, bf16[1,1440,720]{2,1,0:T(8,128)(2,1)S(1)} %copy-done.3), kind=kOutput, calls=%fused_computation.3 | convolution fusion | flops 1459814400 | bytes 6128640 | tf_op jit(solution)/shard_map/dot_general | solution.py:10
  67.2 0.0 copy-done
  67.2 8.6 %convolution_convert_fusion = bf16[704,1440]{1,0:T(8,128)(2,1)} fusion(bf16[1,1440,720]{2,1,0:T(8,128)(2,1)S(1)} %copy-done, f32[704,720]{1,0:T(8,128)} %fusion.1, bf16[704,1440]{1,0:T(8,128)(2,1)} %bitcast.41, bf16[1,1440,720]{2,1,0:T(8,128)(2,1)} %param.10), kind=kOutput, calls=%fused_computation | convolution fusion | flops 2924697600 | bytes 10229760 | tf_op jit(solution)/shard_map/dot_general | solution.py:13
  75.8 0.0 copy-start.2
  75.8 4.5 %all-to-all-start.1 = ((bf16[8,88,1440]{2,1,0:T(8,128)(2,1)}), bf16[8,88,1440]{2,1,0:T(8,128)(2,1)}, u32[]{:S(2)}, u32[]{:S(2)}) async-start(bf16[8,88,1440]{2,1,0:T(8,128)(2,1)} %bitcast.39), calls=%async_computation.1 | async-start | bytes 4325376 | tf_op jit(solution)/shard_map/all_to_all | solution.py:52
  80.3 0.0 copy-done.2
  80.3 0.2 select_reduce_fusion
  80.5 48.5 %all-to-all-done.1 = bf16[8,88,1440]{2,1,0:T(8,128)(2,1)} async-done(((bf16[8,88,1440]{2,1,0:T(8,128)(2,1)}), bf16[8,88,1440]{2,1,0:T(8,128)(2,1)}, u32[]{:S(2)}, u32[]{:S(2)}) %all-to-all-start.1) | async-done | bytes 2027552 | tf_op jit(solution)/shard_map/all_to_all | solution.py:52
  129.0 4.7 %copy.76 = bf16[8,88,1440]{1,0,2:T(8,128)(2,1)} copy(bf16[8,88,1440]{2,1,0:T(8,128)(2,1)} %all-to-all-done.1) | data formatting | bytes 4055040 | tf_op jit(solution)/shard_map/all_to_all | solution.py:52
  133.8 10.1 %all_to_all.26 = bf16[8,88,1440]{1,0,2:T(8,128)(2,1)} all-to-all(bf16[8,88,1440]{1,0,2:T(8,128)(2,1)} %copy.76), channel_id=1, replica_groups=mesh['groups'=2,'seq'=4,'ep'=2,'tp'=2] {'tp'}, dimensions={2} | all-to-all | bytes 4055040 | tf_op jit(solution)/shard_map/all_to_all | solution.py:51
  143.8 6.2 %copy.77 = bf16[2,8,88,720]{3,0,2,1:T(2,128)(2,1)} copy(bf16[2,8,88,720]{2,1,3,0:T(8,128)(2,1)} %bitcast.35) | data formatting | bytes 4055040 | tf_op jit(solution)/shard_map/all_to_all | solution.py:51
  150.0 5.2 %bitcast_reduce_fusion = bf16[2,4,88,720]{3,0,2,1:T(2,128)(2,1)S(1)} fusion(bf16[2,8,88,720]{3,0,2,1:T(2,128)(2,1)} %copy.77), kind=kLoop, calls=%fused_computation.7 | loop fusion | flops 506880 | bytes 3041280 | tf_op jit(solution)/shard_map/reduce_sum | solution.py:59
  155.2 0.1 copy.78
  155.3 2.0 %convolution_convert_fusion.2 = bf16[128,720]{0,1:T(8,128)(2,1)} fusion(f32[128,704]{0,1:T(8,128)S(1)} %select_reduce_fusion, bf16[704,720]{1,0:T(8,128)(2,1)S(1)} %bitcast.37), kind=kOutput, calls=%fused_computation.11 | convolution fusion | flops 778659840 | bytes 1558528 | tf_op jit(solution)/shard_map/dot_general | solution.py:61
  (4 shorter events, 0.0 us)
Async XLA Ops:
  0.0 67.2 %copy-start = (bf16[1,1440,720]{2,1,0:T(8,128)(2,1)S(1)}, bf16[1,1440,720]{2,1,0:T(8,128)(2,1)}, u32[]{:S(2)}) copy-start(bf16[1,1440,720]{2,1,0:T(8,128)(2,1)} %param.11) | copy-start | bytes 6220804
  5.3 58.8 %copy-start.3 = (bf16[1,1440,720]{2,1,0:T(8,128)(2,1)S(1)}, bf16[1,1440,720]{2,1,0:T(8,128)(2,1)}, u32[]{:S(2)}) copy-start(bf16[1,1440,720]{2,1,0:T(8,128)(2,1)} %param.9) | copy-start | bytes 6220804
  62.7 1.3 copy-start.1
  75.8 4.5 %copy-start.2 = (s32[128,4]{0,1:T(4,128)S(1)}, s32[128,4]{0,1:T(4,128)}, u32[]{:S(2)}) copy-start(s32[128,4]{0,1:T(4,128)} %param.8) | copy-start | bytes 6148
  75.8 53.2 %all-to-all-start.1 = ((bf16[8,88,1440]{2,1,0:T(8,128)(2,1)}), bf16[8,88,1440]{2,1,0:T(8,128)(2,1)}, u32[]{:S(2)}, u32[]{:S(2)}) async-start(bf16[8,88,1440]{2,1,0:T(8,128)(2,1)} %bitcast.39), calls=%async_computation.1 | async-start | bytes 4325376 | tf_op jit(solution)/shard_map/all_to_all | solution.py:52
where the time goes:
time: 158 us; the launch traced here: 157 us
  blocking collectives  67.5 us (43%)
  waiting for transfers between devices  48.5 us (31%)
  matrix products  15.2 us (10%)
  local copies, waits for them, and re-layouts  14.1 us (9%)
  other arithmetic  7.45 us (5%)
  starting transfers between devices  4.5 us (3%)
    all_to_all x1, blocking collectives, local(): lax.all_to_all(copied, ('seq', 'ep'), split_axis=0, concat_axis=0, tiled=...  57.4 us
    all_to_all x1, waiting for transfers between devices, local(): lax.all_to_all(slice_rows, ('seq', 'ep'), split_axis=0, concat_axis=0, ti...  48.5 us
    all_to_all x1, blocking collectives, local(): lax.all_to_all(lax.all_to_all(slice_rows, ('seq', 'ep'), split_axis=0, co...  10.1 us
    dot_general x1, matrix products, slice_output(): lax.dot_general(activation, down_cols, (((1,), (1,)), ((), ())), preferre...  8.55 us
    all_to_all x1, local copies, waits for them, and re-layouts, local(): lax.all_to_all(lax.all_to_all(slice_rows, ('seq', 'ep'), split_axis=0, co...  6.16 us
    reduce_sum x1, other arithmetic, local(): jnp.sum(came_back.astype(jnp.float32), axis=2).astype(jnp.bfloat16)  5.2 us
    all_to_all x1, local copies, waits for them, and re-layouts, local(): lax.all_to_all(slice_rows, ('seq', 'ep'), split_axis=0, concat_axis=0, ti...  4.73 us
    all_to_all x1, starting transfers between devices, local(): lax.all_to_all(slice_rows, ('seq', 'ep'), split_axis=0, concat_axis=0, ti...  4.5 us
  transfers between devices with their start and end apart: 1, of which 1 were waited for; matrix products, arithmetic and copies ran while one was open for 0% of the time, Pallas kernels for 0%

commit v1 on v0

--- a/solution.py
+++ b/solution.py
@@ -2,6 +2,7 @@
 import jax.numpy as jnp
 from jax import lax
 from jax.sharding import PartitionSpec as P
+from jax.lax import axis_index, ppermute, psum
 
 TOP = 4
 
@@ -45,7 +46,27 @@
     combiner = jnp.sum(combiner.reshape(token_count, TOP, -1), axis=1)
     copied = jnp.broadcast_to(outgoing[:, None], (seq_count, ep_count, capacity, model_width))
     copied = copied.reshape(seq_count * ep_count, capacity, model_width)
-    arrived = lax.all_to_all(copied, ("seq", "ep"), split_axis=0, concat_axis=0, tiled=True)
+
+    def use_patches(content):
+        current_value = psum(1, ("seq", "ep"))
+        shaped, a_next = (current_value, axis_index(("seq", "ep")))
+        r1 = content.shape[0] // shaped
+        tile_out = list(content.shape)
+        tile_out[0] = r1
+        known = tile_out[0]
+        tile_out[0] = known * shaped
+        answer = jnp.zeros(tile_out, content.dtype)
+        for w in range(shaped):
+            opened = lax.dynamic_slice_in_dim(content, (a_next ^ w) * r1, r1, axis=0)
+            if w:
+                reached = range(shaped)
+                later = map(lambda p: (p, p ^ w), reached)
+                current_block = list(later)
+                opened = ppermute(opened, ("seq", "ep"), current_block)
+            answer = lax.dynamic_update_slice_in_dim(answer, opened, (a_next ^ w) * known, axis=0)
+        return answer
+
+    arrived = use_patches(copied)
     slice_rows = slice_output(arrived.reshape(-1, model_width), w_gate[0], w_up[0], w_down[0])
     slice_rows = slice_rows.reshape(seq_count * ep_count, capacity, model_width)
     came_back = lax.all_to_all(

time: 158 us -> 156 us (0.987)
  blocking collectives: 67.5 us -> 10.1 us
  waiting for transfers between devices: 48.5 us -> 80.1 us
  starting transfers between devices: 4.5 us -> 27.5 us
    all_to_all x1 -> x0, blocking collectives: 57.4 us -> none  [local(): lax.all_to_all(copied, ('seq', 'ep'), split_axis=0, concat_axis=0, tiled=...]
    ppermute x0 -> x7, waiting for transfers between devices: none -> 31.3 us  [use_patches(): opened = ppermute(opened, ('seq', 'ep'), current_block)]
    ppermute x0 -> x7, starting transfers between devices: none -> 13.8 us  [use_patches(): opened = ppermute(opened, ('seq', 'ep'), current_block)]
    all_to_all x1, starting transfers between devices: 4.5 us -> 13.7 us  [local(): lax.all_to_all(slice_rows, ('seq', 'ep'), split_axis=0, concat_axis=0, ti...]
  transfers between devices with their start and end apart: 1 -> 8, of which waited for: 1 -> 5; matrix products, arithmetic and copies ran while one was open for 0% -> 0% of each run, Pallas kernels for 0% -> 0%
where the time goes in v1:
time: 156 us; the launch traced here: 155 us
  waiting for transfers between devices  80.1 us (51%)
  starting transfers between devices  27.5 us (18%)
  matrix products  15.2 us (10%)
  local copies, waits for them, and re-layouts  14.5 us (9%)
  blocking collectives  10.1 us (6%)
  other arithmetic  7.45 us (5%)
    all_to_all x1, waiting for transfers between devices, local(): lax.all_to_all(slice_rows, ('seq', 'ep'), split_axis=0, concat_axis=0, ti...  48.8 us
    ppermute x7, waiting for transfers between devices, use_patches(): opened = ppermute(opened, ('seq', 'ep'), current_block)  31.3 us
    ppermute x7, starting transfers between devices, use_patches(): opened = ppermute(opened, ('seq', 'ep'), current_block)  13.8 us
    all_to_all x1, starting transfers between devices, local(): lax.all_to_all(slice_rows, ('seq', 'ep'), split_axis=0, concat_axis=0, ti...  13.7 us
    all_to_all x1, blocking collectives, local(): lax.all_to_all(lax.all_to_all(slice_rows, ('seq', 'ep'), split_axis=0, co...  10.1 us
    dot_general x1, matrix products, slice_output(): lax.dot_general(activation, down_cols, (((1,), (1,)), ((), ())), preferre...  8.59 us
    all_to_all x1, local copies, waits for them, and re-layouts, local(): lax.all_to_all(lax.all_to_all(slice_rows, ('seq', 'ep'), split_axis=0, co...  6.16 us
    reduce_sum x1, other arithmetic, local(): jnp.sum(came_back.astype(jnp.float32), axis=2).astype(jnp.bfloat16)  5.2 us
  transfers between devices with their start and end apart: 8, of which 5 were waited for; matrix products, arithmetic and copies ran while one was open for 0% of the time, Pallas kernels for 0%

profile of v1, /device:TPU:0, one launch (start us, length us, event | category | flops | bytes accessed | tf_op | source)
XLA Modules:
  0.0 155.1 jit_solution(8149848130515577488)
XLA Ops:
  0.0 0.0 copy-start
  0.0 0.9 copy.72
  0.9 0.1 eq.70
  1.0 0.1 eq.66
  1.2 1.1 reduce-window.6
  2.3 0.2 slice_reduce_fusion
  2.6 0.1 fusion.10
  2.7 0.1 reduce_sum.33
  2.8 0.1 copy.74
  2.8 0.7 add_select_fusion.2
  3.6 0.1 fusion.9
  3.7 1.4 convolution_convert_fusion.1
  5.1 0.2 broadcast_in_dim.34
  5.3 0.1 broadcast_in_dim.32
  5.5 0.2 constant_dynamic-slice_fusion
  5.7 0.0 copy-start.3
  5.7 3.0 %collective-permute-start = (bf16[1,88,1440]{2,1,0:T(8,128)(2,1)S(1)}, bf16[1,88,1440]{2,1,0:T(8,128)(2,1)S(1)}, u32[]{:S(2)}, u32[]{:S(2)}) collective-permute-start(bf16[1,88,1440]{2,1,0:T(8,128)(2,1)S(1)} %get-tuple-element.11), channel_id=1, source_target_pairs={{0,2},{2,0},{4,6},{6,4},{8,10},{10,8},{12,14},{14,12},{1,3},{3,1},... | collective-permute-start | bytes 760328 | tf_op jit(solution)/shard_map/ppermute | solution.py:65
  8.7 1.6 %collective-permute-start.1 = (bf16[1,88,1440]{2,1,0:T(8,128)(2,1)S(1)}, bf16[1,88,1440]{2,1,0:T(8,128)(2,1)S(1)}, u32[]{:S(2)}, u32[]{:S(2)}) collective-permute-start(bf16[1,88,1440]{2,1,0:T(8,128)(2,1)S(1)} %get-tuple-element.10), channel_id=1, source_target_pairs={{0,4},{2,6},{4,0},{6,2},{8,12},{10,14},{12,8},{14,10},{1,5},{3,7},... | collective-permute-start | bytes 760328 | tf_op jit(solution)/shard_map/ppermute | solution.py:65
  10.3 0.0 collective-permute-start.2
  10.3 3.0 %collective-permute-start.3 = (bf16[1,88,1440]{2,1,0:T(8,128)(2,1)S(1)}, bf16[1,88,1440]{2,1,0:T(8,128)(2,1)S(1)}, u32[]{:S(2)}, u32[]{:S(2)}) collective-permute-start(bf16[1,88,1440]{2,1,0:T(8,128)(2,1)S(1)} %get-tuple-element.8), channel_id=1, source_target_pairs={{0,8},{2,10},{4,12},{6,14},{8,0},{10,2},{12,4},{14,6},{1,9},{3,11}... | collective-permute-start | bytes 760328 | tf_op jit(solution)/shard_map/ppermute | solution.py:65
  13.3 1.3 collective-permute-start.4
  14.5 0.6 collective-permute-done
  15.2 3.9 %collective-permute-start.5 = (bf16[1,88,1440]{2,1,0:T(8,128)(2,1)S(1)}, bf16[1,88,1440]{2,1,0:T(8,128)(2,1)S(1)}, u32[]{:S(2)}, u32[]{:S(2)}) collective-permute-start(bf16[1,88,1440]{2,1,0:T(8,128)(2,1)S(1)} %get-tuple-element.6), channel_id=1, source_target_pairs={{0,12},{2,14},{4,8},{6,10},{8,4},{10,6},{12,0},{14,2},{1,13},{3,15... | collective-permute-start | bytes 760328 | tf_op jit(solution)/shard_map/ppermute | solution.py:65
  19.1 9.7 %collective-permute-done.1 = bf16[1,88,1440]{2,1,0:T(8,128)(2,1)S(1)} collective-permute-done((bf16[1,88,1440]{2,1,0:T(8,128)(2,1)S(1)}, bf16[1,88,1440]{2,1,0:T(8,128)(2,1)S(1)}, u32[]{:S(2)}, u32[]{:S(2)}) %collective-permute-start.1) | collective-permute-done | bytes 253472 | tf_op jit(solution)/shard_map/ppermute | solution.py:65
  28.7 1.1 collective-permute-start.6
  29.8 2.5 %collective-permute-done.2 = bf16[1,88,1440]{2,1,0:T(8,128)(2,1)S(1)} collective-permute-done((bf16[1,88,1440]{2,1,0:T(8,128)(2,1)S(1)}, bf16[1,88,1440]{2,1,0:T(8,128)(2,1)S(1)}, u32[]{:S(2)}, u32[]{:S(2)}) %collective-permute-start.2) | collective-permute-done | bytes 253472 | tf_op jit(solution)/shard_map/ppermute | solution.py:65
  32.3 0.0 collective-permute-done.3
  32.3 18.5 %collective-permute-done.4 = bf16[1,88,1440]{2,1,0:T(8,128)(2,1)S(1)} collective-permute-done((bf16[1,88,1440]{2,1,0:T(8,128)(2,1)S(1)}, bf16[1,88,1440]{2,1,0:T(8,128)(2,1)S(1)}, u32[]{:S(2)}, u32[]{:S(2)}) %collective-permute-start.4) | collective-permute-done | bytes 253472 | tf_op jit(solution)/shard_map/ppermute | solution.py:65
  50.9 0.0 collective-permute-done.5
  50.9 0.0 collective-permute-done.6
  51.0 0.0 copy-start.1
  51.0 1.3 copy-done.1
  52.3 0.0 copy-done.3
  52.3 3.2 %fusion.3 = f32[704,720]{1,0:T(8,128)} fusion(bf16[704,1440]{1,0:T(8,128)(2,1)S(1)} %bitcast.39, bf16[1,1440,720]{2,1,0:T(8,128)(2,1)S(1)} %copy-done.3), kind=kOutput, calls=%fused_computation.5 | convolution fusion | flops 1459814400 | bytes 6128640 | tf_op jit(solution)/shard_map/dot_general | solution.py:12
  55.5 0.0 copy-done
  55.5 8.6 %convolution_convert_fusion = bf16[704,1440]{1,0:T(8,128)(2,1)} fusion(bf16[1,1440,720]{2,1,0:T(8,128)(2,1)S(1)} %copy-done, f32[704,720]{1,0:T(8,128)} %fusion.3, bf16[704,1440]{1,0:T(8,128)(2,1)} %bitcast.40, bf16[1,1440,720]{2,1,0:T(8,128)(2,1)} %param.9), kind=kOutput, calls=%fused_computation | convolution fusion | flops 2924697600 | bytes 10229760 | tf_op jit(solution)/shard_map/dot_general | solution.py:14
  64.1 0.0 copy-start.2
  64.1 13.7 %all-to-all-start = ((bf16[8,88,1440]{2,1,0:T(8,128)(2,1)}), bf16[8,88,1440]{2,1,0:T(8,128)(2,1)}, u32[]{:S(2)}, u32[]{:S(2)}) async-start(bf16[8,88,1440]{2,1,0:T(8,128)(2,1)} %bitcast.41), calls=%async_computation | async-start | bytes 4325376 | tf_op jit(solution)/shard_map/all_to_all | solution.py:73
  77.7 0.0 copy-done.2
  77.8 0.2 select_reduce_fusion
  77.9 48.8 %all-to-all-done = bf16[8,88,1440]{2,1,0:T(8,128)(2,1)} async-done(((bf16[8,88,1440]{2,1,0:T(8,128)(2,1)}), bf16[8,88,1440]{2,1,0:T(8,128)(2,1)}, u32[]{:S(2)}, u32[]{:S(2)}) %all-to-all-start) | async-done | bytes 2027552 | tf_op jit(solution)/shard_map/all_to_all | solution.py:73
  126.8 4.7 %copy.76 = bf16[8,88,1440]{1,0,2:T(8,128)(2,1)} copy(bf16[8,88,1440]{2,1,0:T(8,128)(2,1)} %all-to-all-done) | data formatting | bytes 4055040 | tf_op jit(solution)/shard_map/all_to_all | solution.py:73
  131.5 10.1 %all_to_all.20 = bf16[8,88,1440]{1,0,2:T(8,128)(2,1)} all-to-all(bf16[8,88,1440]{1,0,2:T(8,128)(2,1)} %copy.76), channel_id=1, replica_groups=mesh['groups'=2,'seq'=4,'ep'=2,'tp'=2] {'tp'}, dimensions={2} | all-to-all | bytes 4055040 | tf_op jit(solution)/shard_map/all_to_all | solution.py:72
  141.5 6.2 %copy.77 = bf16[2,8,88,720]{3,0,2,1:T(2,128)(2,1)} copy(bf16[2,8,88,720]{2,1,3,0:T(8,128)(2,1)} %bitcast.35) | data formatting | bytes 4055040 | tf_op jit(solution)/shard_map/all_to_all | solution.py:72
  147.7 5.2 %bitcast_reduce_fusion = bf16[2,4,88,720]{3,0,2,1:T(2,128)(2,1)S(1)} fusion(bf16[2,8,88,720]{3,0,2,1:T(2,128)(2,1)} %copy.77), kind=kLoop, calls=%fused_computation.7 | loop fusion | flops 506880 | bytes 3041280 | tf_op jit(solution)/shard_map/reduce_sum | solution.py:80
  152.9 0.1 copy.78
  153.0 2.0 %convolution_convert_fusion.2 = bf16[128,720]{0,1:T(8,128)(2,1)} fusion(f32[128,704]{0,1:T(8,128)S(1)} %select_reduce_fusion, bf16[704,720]{1,0:T(8,128)(2,1)S(1)} %bitcast.37), kind=kOutput, calls=%fused_computation.11 | convolution fusion | flops 778659840 | bytes 1558528 | tf_op jit(solution)/shard_map/dot_general | solution.py:82
  (11 shorter events, 0.2 us)
Async XLA Ops:
  0.0 55.5 %copy-start = (bf16[1,1440,720]{2,1,0:T(8,128)(2,1)S(1)}, bf16[1,1440,720]{2,1,0:T(8,128)(2,1)}, u32[]{:S(2)}) copy-start(bf16[1,1440,720]{2,1,0:T(8,128)(2,1)} %param.11) | copy-start | bytes 6220804
  5.7 46.6 %copy-start.3 = (bf16[1,1440,720]{2,1,0:T(8,128)(2,1)S(1)}, bf16[1,1440,720]{2,1,0:T(8,128)(2,1)}, u32[]{:S(2)}) copy-start(bf16[1,1440,720]{2,1,0:T(8,128)(2,1)} %param.10) | copy-start | bytes 6220804
  5.7 9.5 %collective-permute-start = (bf16[1,88,1440]{2,1,0:T(8,128)(2,1)S(1)}, bf16[1,88,1440]{2,1,0:T(8,128)(2,1)S(1)}, u32[]{:S(2)}, u32[]{:S(2)}) collective-permute-start(bf16[1,88,1440]{2,1,0:T(8,128)(2,1)S(1)} %get-tuple-element.11), channel_id=1, source_target_pairs={{0,2},{2,0},{4,6},{6,4},{8,10},{10,8},{12,14},{14,12},{1,3},{3,1},... | collective-permute-start | bytes 760328 | tf_op jit(solution)/shard_map/ppermute | solution.py:65
  8.7 20.0 %collective-permute-start.1 = (bf16[1,88,1440]{2,1,0:T(8,128)(2,1)S(1)}, bf16[1,88,1440]{2,1,0:T(8,128)(2,1)S(1)}, u32[]{:S(2)}, u32[]{:S(2)}) collective-permute-start(bf16[1,88,1440]{2,1,0:T(8,128)(2,1)S(1)} %get-tuple-element.10), channel_id=1, source_target_pairs={{0,4},{2,6},{4,0},{6,2},{8,12},{10,14},{12,8},{14,10},{1,5},{3,7},... | collective-permute-start | bytes 760328 | tf_op jit(solution)/shard_map/ppermute | solution.py:65
  10.3 22.0 %collective-permute-start.2 = (bf16[1,88,1440]{2,1,0:T(8,128)(2,1)S(1)}, bf16[1,88,1440]{2,1,0:T(8,128)(2,1)S(1)}, u32[]{:S(2)}, u32[]{:S(2)}) collective-permute-start(bf16[1,88,1440]{2,1,0:T(8,128)(2,1)S(1)} %get-tuple-element.9), channel_id=1, source_target_pairs={{0,6},{2,4},{4,2},{6,0},{8,14},{10,12},{12,10},{14,8},{1,7},{3,5},... | collective-permute-start | bytes 760328 | tf_op jit(solution)/shard_map/ppermute | solution.py:65
  10.3 22.0 %collective-permute-start.3 = (bf16[1,88,1440]{2,1,0:T(8,128)(2,1)S(1)}, bf16[1,88,1440]{2,1,0:T(8,128)(2,1)S(1)}, u32[]{:S(2)}, u32[]{:S(2)}) collective-permute-start(bf16[1,88,1440]{2,1,0:T(8,128)(2,1)S(1)} %get-tuple-element.8), channel_id=1, source_target_pairs={{0,8},{2,10},{4,12},{6,14},{8,0},{10,2},{12,4},{14,6},{1,9},{3,11}... | collective-permute-start | bytes 760328 | tf_op jit(solution)/shard_map/ppermute | solution.py:65
  13.3 37.5 %collective-permute-start.4 = (bf16[1,88,1440]{2,1,0:T(8,128)(2,1)S(1)}, bf16[1,88,1440]{2,1,0:T(8,128)(2,1)S(1)}, u32[]{:S(2)}, u32[]{:S(2)}) collective-permute-start(bf16[1,88,1440]{2,1,0:T(8,128)(2,1)S(1)} %get-tuple-element.7), channel_id=1, source_target_pairs={{0,10},{2,8},{4,14},{6,12},{8,2},{10,0},{12,6},{14,4},{1,11},{3,9}... | collective-permute-start | bytes 760328 | tf_op jit(solution)/shard_map/ppermute | solution.py:65
  15.2 35.7 %collective-permute-start.5 = (bf16[1,88,1440]{2,1,0:T(8,128)(2,1)S(1)}, bf16[1,88,1440]{2,1,0:T(8,128)(2,1)S(1)}, u32[]{:S(2)}, u32[]{:S(2)}) collective-permute-start(bf16[1,88,1440]{2,1,0:T(8,128)(2,1)S(1)} %get-tuple-element.6), channel_id=1, source_target_pairs={{0,12},{2,14},{4,8},{6,10},{8,4},{10,6},{12,0},{14,2},{1,13},{3,15... | collective-permute-start | bytes 760328 | tf_op jit(solution)/shard_map/ppermute | solution.py:65
  28.7 22.2 %collective-permute-start.6 = (bf16[1,88,1440]{2,1,0:T(8,128)(2,1)S(1)}, bf16[1,88,1440]{2,1,0:T(8,128)(2,1)S(1)}, u32[]{:S(2)}, u32[]{:S(2)}) collective-permute-start(bf16[1,88,1440]{2,1,0:T(8,128)(2,1)S(1)} %get-tuple-element.5), channel_id=1, source_target_pairs={{0,14},{2,12},{4,10},{6,8},{8,6},{10,4},{12,2},{14,0},{1,15},{3,13... | collective-permute-start | bytes 760328 | tf_op jit(solution)/shard_map/ppermute | solution.py:65
  51.0 1.3 copy-start.1
  64.1 13.7 %copy-start.2 = (s32[128,4]{0,1:T(4,128)S(1)}, s32[128,4]{0,1:T(4,128)}, u32[]{:S(2)}) copy-start(s32[128,4]{0,1:T(4,128)} %param.8) | copy-start | bytes 6148
  64.1 62.7 %all-to-all-start = ((bf16[8,88,1440]{2,1,0:T(8,128)(2,1)}), bf16[8,88,1440]{2,1,0:T(8,128)(2,1)}, u32[]{:S(2)}, u32[]{:S(2)}) async-start(bf16[8,88,1440]{2,1,0:T(8,128)(2,1)} %bitcast.41), calls=%async_computation | async-start | bytes 4325376 | tf_op jit(solution)/shard_map/all_to_all | solution.py:73
